TPU v7x, 128 devices: a whole 4x4x4 slice. The times are simulated.
128 devices in a mesh: req: 32 (over y, z, core), tensor: 4 (over x).
Axes of the slice: x: 4, y: 4, z: 4, core: 2. Of those that a mesh axis runs over, the one named last changes fastest.
Arguments:
- hidden: bfloat16 [32768, 1024], P('req', 'tensor')
- gain: bfloat16 [1024], P('tensor'), may hold values from 0.5 to 1.5
- head: bfloat16 [1024, 32128], P(None, ('req', 'tensor'))
- token_ids: int32 [32768], P('req'), may hold values from 0 to 32127
- lengths: int32 [32], P('req'), may hold values from 1 to 1024, 12288 in all
- prompt_of: int32 [32], P('req'), may hold values from 0 to 3, as said below
Outputs:
- token_logprob: float32 [32768], P(('req', 'tensor'))
- token_entropy: float32 [32768], P(('req', 'tensor'))
- prompt_stats: float32 [4, 2], replicated
Inputs may be any that keep to these rules, and one draw needn't show every extreme that they name: The lengths sum to 12288 and the longest is exactly 1024. `prompt_of`: a prompt may have no responses.
All inputs are finite; a program needn't handle non-finite values. No bound on the sum of `lengths` on one device may be relied on, other than what follows from the above.
Results may differ from a plain program's by a relative error of at most 0.0019.
Values may be sent and summed in bfloat16 or wider, within the bound.
A program may use at most 128 MiB of HBM per device.

v0:
```python
import functools

import jax
import jax.numpy as jnp
from jax import lax
from jax.experimental import pallas as pl
from jax.experimental.pallas import tpu as pltpu
from jax.sharding import Mesh, PartitionSpec as P
from jax.experimental.layout import Layout, with_layout_constraint

PROMPTS = 4
REQ = ("y", "z", "c")
MESH_AXES = ("y", "z", "c", "x")
NEG = -1e30
SUB = 8

eps = 1e-06


def peer_kernel(n, coords_of, x_ref, o_ref, held, send_sem, recv_sem):
    me, coords = coords_of()
    barrier = pltpu.get_barrier_semaphore()
    for d in range(1, n):
        pl.semaphore_signal(barrier, inc=1, device_id=coords((me + d) % n), device_id_type=pl.DeviceIdType.MESH)
    pl.semaphore_wait(barrier, n - 1)
    held[pl.ds(me, 1)] = x_ref[...][None]
    copies = []
    for d in range(1, n):
        c = pltpu.make_async_remote_copy(
            src_ref=x_ref, dst_ref=held.at[me], send_sem=send_sem.at[d], recv_sem=recv_sem.at[d],
            device_id=coords((me + d) % n), device_id_type=pl.DeviceIdType.MESH)
        c.start()
        copies.append(c)
    for c in copies:
        c.wait()
    o_ref[...] = held[...]


def peer_gather(x, n, coords_of, cid):
    return pl.pallas_call(
        functools.partial(peer_kernel, n, coords_of),
        out_shape=jax.ShapeDtypeStruct((n,) + x.shape, x.dtype),
        in_specs=[pl.BlockSpec(memory_space=pltpu.VMEM)],
        out_specs=pl.BlockSpec(memory_space=pltpu.VMEM),
        scratch_shapes=[pltpu.VMEM((n,) + x.shape, x.dtype), pltpu.SemaphoreType.DMA((n,)), pltpu.SemaphoreType.DMA((n,))],
        compiler_params=pltpu.CompilerParams(collective_id=cid, has_side_effects=True),
    )(x)


def along_x():
    here = tuple(lax.axis_index(name) for name in MESH_AXES)
    return here[3], lambda t: here[:3] + (t,)


def along_req():
    here = tuple(lax.axis_index(name) for name in MESH_AXES)
    zs, cs = lax.axis_size("z"), lax.axis_size("c")
    me = (here[0] * zs + here[1]) * cs + here[2]
    return me, lambda t: (t // (zs * cs), (t // cs) % zs, t % cs, here[3])


def stats_kernel(steps, w_ref, x_ref, b_ref, v_ref, t_ref, top_ref, tot_ref, mom_ref, pick_ref, m_sc, s_sc, mo_sc, p_sc):
    j = pl.program_id(1)

    @pl.when(j == 0)
    def _():
        m_sc[...] = jnp.full(m_sc.shape, NEG, jnp.float32)
        s_sc[...] = jnp.zeros(s_sc.shape, jnp.float32)
        mo_sc[...] = jnp.zeros(mo_sc.shape, jnp.float32)
        p_sc[...] = jnp.zeros(p_sc.shape, jnp.float32)

    logits = jnp.dot(w_ref[...], x_ref[...], preferred_element_type=jnp.float32)
    logits = logits + b_ref[...]
    tn, tm = logits.shape
    grouped = logits.reshape(tn // SUB, SUB, tm)
    m_old = m_sc[...]
    m_new = jnp.maximum(m_old, jnp.max(jnp.max(grouped, axis=0), axis=0, keepdims=True))
    alpha = jnp.exp(m_old - m_new)
    e = jnp.exp(logits - m_new)
    hit = jnp.where(v_ref[...] == t_ref[...], logits, 0.0)
    s_sc[...] = s_sc[...] * alpha + jnp.sum(e.reshape(tn // SUB, SUB, tm), axis=0)
    mo_sc[...] = mo_sc[...] * alpha + jnp.sum((e * logits).reshape(tn // SUB, SUB, tm), axis=0)
    p_sc[...] = p_sc[...] + jnp.sum(hit.reshape(tn // SUB, SUB, tm), axis=0)
    m_sc[...] = m_new

    @pl.when(j == steps - 1)
    def _():
        top_ref[...] = m_sc[...]
        tot_ref[...] = jnp.sum(s_sc[...], axis=0, keepdims=True)
        mom_ref[...] = jnp.sum(mo_sc[...], axis=0, keepdims=True)
        pick_ref[...] = jnp.sum(p_sc[...], axis=0, keepdims=True)


def fused_stats(normed_t, piece, bias, vocab_ids, ids, tm=1024, tn=1024):
    depth, rows = normed_t.shape
    cols = piece.shape[0]
    grid = (rows // tm, cols // tn)
    stat = jax.ShapeDtypeStruct((1, rows), jnp.float32)
    stat_spec = pl.BlockSpec((1, tm), lambda i, j: (0, i))
    return pl.pallas_call(
        functools.partial(stats_kernel, grid[1]),
        out_shape=(stat, stat, stat, stat),
        grid=grid,
        in_specs=[
            pl.BlockSpec((tn, depth), lambda i, j: (j, 0)),
            pl.BlockSpec((depth, tm), lambda i, j: (0, i)),
            pl.BlockSpec((tn, 1), lambda i, j: (j, 0)),
            pl.BlockSpec((tn, 1), lambda i, j: (j, 0)),
            pl.BlockSpec((1, tm), lambda i, j: (0, i)),
        ],
        out_specs=(stat_spec, stat_spec, stat_spec, stat_spec),
        scratch_shapes=[pltpu.VMEM((1, tm), jnp.float32)] + [pltpu.VMEM((SUB, tm), jnp.float32)] * 3,
        compiler_params=pltpu.CompilerParams(dimension_semantics=("arbitrary", "arbitrary")),
        cost_estimate=pl.CostEstimate(
            flops=2 * rows * cols * depth,
            transcendentals=rows * cols,
            bytes_accessed=2 * (rows * depth + grid[0] * cols * depth),
        ),
    )(piece, normed_t, bias, vocab_ids, ids)


def chunk_stats(normed, piece, valid, vocab_ids, ids):
    bias = jnp.where(valid, 0.0, NEG).astype(jnp.float32)[:, None]
    top, total, moment, pick = fused_stats(normed.T, piece, bias, vocab_ids[:, None], ids[None, :])
    return top[0], total[0], moment[0], pick[0]


def merge(stats):
    tops = jnp.stack([s[0] for s in stats])
    top = jnp.max(tops, axis=0)
    factor = jnp.exp(tops - top[None, :])
    total = jnp.sum(factor * jnp.stack([s[1] for s in stats]), axis=0)
    moment = jnp.sum(factor * jnp.stack([s[2] for s in stats]), axis=0)
    pick = jnp.sum(jnp.stack([s[3] for s in stats]), axis=0)
    return top, total, moment, pick


def body(hidden, gain, head, token_ids, lengths, prompt_of):
    rows, part_width = hidden.shape
    splits = lax.axis_size("x")
    column_index = lax.axis_index("x")
    req_count = lax.axis_size(REQ)
    shard_cols = head.shape[1]
    width = part_width * splits

    extra = jnp.zeros((8, part_width), hidden.dtype).at[0].set(gain)
    packed = jnp.concatenate([hidden, extra], axis=0)
    shift = lambda x, d: lax.ppermute(x, "x", [(i, (i + d) % splits) for i in range(splits)])
    from_left = shift(packed, 1)
    from_right = shift(packed, -1)
    from_far = shift(from_left, 1)
    stacked = jnp.stack([packed, from_right, from_far, from_left])
    order = (jnp.arange(splits, dtype=jnp.int32) - column_index) % splits
    stacked = jnp.take(stacked, order, axis=0)
    gathered = jnp.transpose(stacked, (1, 0, 2)).reshape(rows + 8, width)
    widened = gathered[:rows].astype(jnp.float32)
    gain_full = gathered[rows].astype(jnp.float32)
    scale = lax.rsqrt(jnp.sum(widened * widened, axis=1) / width + eps)
    normed = (widened * scale[:, None] * gain_full[None, :]).astype(jnp.bfloat16)

    chunk = 256
    bounds = [(lo, min(lo + chunk, shard_cols)) for lo in range(0, shard_cols, chunk)]
    stats = []
    for lo, hi in bounds:
        part = head[:, lo:hi].T
        if hi - lo < chunk:
            part = jnp.concatenate([part, jnp.zeros((chunk - (hi - lo), part.shape[1]), part.dtype)], axis=0)
        part = with_layout_constraint(part, Layout(major_to_minor=(0, 1)))
        piece = lax.all_gather(part, REQ, axis=0, tiled=False)
        piece = with_layout_constraint(piece, Layout(major_to_minor=(0, 1, 2)))
        piece = piece.reshape(req_count * chunk, piece.shape[2])
        g = jnp.arange(req_count * chunk, dtype=jnp.int32)
        owner = g // chunk
        offset = lo + g % chunk
        valid = offset < hi
        vocab_ids = jnp.where(valid, (owner * splits + column_index) * shard_cols + offset, -1)
        stats.append(chunk_stats(normed, piece, valid, vocab_ids, token_ids))
    mine = merge(stats)

    everyone = peer_gather(jnp.stack(mine), splits, along_x, 0)
    top, total, moment, picked = merge([tuple(everyone[k, j] for j in range(4)) for k in range(splits)])

    positions = jnp.arange(rows, dtype=jnp.int32)
    live = positions < lengths[0]
    safe_total = jnp.where(live, total, 1.0)
    log_norm = top + jnp.log(safe_total)
    logprob = jnp.where(live, picked - log_norm, 0.0)
    entropy = jnp.where(live, log_norm - moment / safe_total, 0.0)
    onehot = (jnp.arange(PROMPTS, dtype=jnp.int32) == prompt_of[0]).astype(jnp.float32)
    share = rows // splits
    own_logprob = lax.dynamic_slice_in_dim(logprob, column_index * share, share)
    own_entropy = lax.dynamic_slice_in_dim(entropy, column_index * share, share)
    summary = jnp.stack([jnp.sum(entropy), jnp.sum(logprob), lengths[0].astype(jnp.float32)])
    summed = jnp.zeros((8, 128), jnp.float32).at[:PROMPTS, :3].set(onehot[:, None] * summary[None, :])
    summed = jnp.sum(peer_gather(summed, req_count, along_req, 1), axis=0)[:PROMPTS, :3]
    prompt_stats = summed[:, :2] / jnp.maximum(summed[:, 2:3], 1.0)
    return (own_logprob, own_entropy, prompt_stats)


def solution(mesh):
    req_axes = mesh.devices.shape[0] // 8
    fine = Mesh(mesh.devices.reshape(req_axes, 4, 2, mesh.devices.shape[1]), ("y", "z", "c", "x"))
    in_specs = (
        P(REQ, "x"),
        P("x"),
        P(None, REQ + ("x",)),
        P(REQ),
        P(REQ),
        P(REQ),
    )
    out_specs = (P(REQ + ("x",)), P(REQ + ("x",)), P())
    return jax.shard_map(body, mesh=fine, in_specs=in_specs, out_specs=out_specs, check_vma=False)
```

profile of v0, /device:TPU:0, one launch (start us, length us, event | category | flops | bytes accessed | tf_op | source)
XLA Modules:
  0.0 154.2 jit_solution(11174550869190573520)
XLA Ops:
  7.2 0.0 all-gather.3.cloned.1.call-start
  7.2 1.2 copy.17
  8.5 0.8 concatenate.10
  9.3 0.0 all-gather.3.cloned.1.call-update
  9.3 0.7 reshape.257
  10.0 1.1 fusion.25
  11.1 1.7 %collective-permute-start.1 = (bf16[1032,256]{1,0:T(8,128)(2,1)S(1)}, bf16[1032,256]{1,0:T(8,128)(2,1)S(1)}, u32[]{:S(2)}, u32[]{:S(2)}) collective-permute-start(bf16[1032,256]{1,0:T(8,128)(2,1)S(1)} %get-tuple-element.51), channel_id=1, source_target_pairs={{0,1},{1,2},{2,3},{3,0},{4,5},{5,6},{6,7},{7,4},{8,9},{9,10},{10,1... | collective-permute-start | bytes 1585160 | tf_op jit(solution)/shard_map/ppermute | solution.py:148
  12.8 1.6 %collective-permute-start = (bf16[1032,256]{1,0:T(8,128)(2,1)S(1)}, bf16[1032,256]{1,0:T(8,128)(2,1)S(1)}, u32[]{:S(2)}, u32[]{:S(2)}) collective-permute-start(bf16[1032,256]{1,0:T(8,128)(2,1)S(1)} %get-tuple-element.51), channel_id=1, source_target_pairs={{0,3},{1,0},{2,1},{3,2},{4,7},{5,4},{6,5},{7,6},{8,11},{9,8},{10,9... | collective-permute-start | bytes 1585160 | tf_op jit(solution)/shard_map/ppermute | solution.py:148
  14.4 2.2 %fusion.13.b_ref = f32[8192,1]{1,0:T(8,128)} fusion(), kind=kLoop, calls=%fused_computation.21 | loop fusion | flops 65536 | bytes 32768 | tf_op jit(solution)/shard_map/jit(_where)/select_n | solution.py:123
  16.6 9.4 %collective-permute-done.1 = bf16[1032,256]{1,0:T(8,128)(2,1)S(1)} collective-permute-done((bf16[1032,256]{1,0:T(8,128)(2,1)S(1)}, bf16[1032,256]{1,0:T(8,128)(2,1)S(1)}, u32[]{:S(2)}, u32[]{:S(2)}) %collective-permute-start.1) | collective-permute-done | bytes 528416 | tf_op jit(solution)/shard_map/ppermute | solution.py:148
  26.1 0.5 collective-permute-start.2
  26.5 5.0 %fusion.5.v_ref = s32[8192,1]{1,0:T(8,128)} fusion(s32[]{:T(128)S(6)} %axis_index.12), kind=kLoop, calls=%fused_computation.10 | loop fusion | flops 147456 | bytes 32772 | tf_op jit(solution)/shard_map/jit(_where)/select_n | solution.py:176
  32.9 0.0 collective-permute-done
  32.9 0.0 copy-start
  32.9 7.2 %collective-permute-done.2 = bf16[1032,256]{1,0:T(8,128)(2,1)S(1)} collective-permute-done((bf16[1032,256]{1,0:T(8,128)(2,1)S(1)}, bf16[1032,256]{1,0:T(8,128)(2,1)S(1)}, u32[]{:S(2)}, u32[]{:S(2)}) %collective-permute-start.2) | collective-permute-done | bytes 528416 | tf_op jit(solution)/shard_map/ppermute | solution.py:148
  40.1 0.0 copy-start.1
  40.1 0.0 copy-done
  40.1 0.8 copy-done.1
  40.9 1.5 pad_maximum_fusion
  42.4 2.1 %gather_fusion = bf16[4,1032,256]{2,1,0:T(8,128)(2,1)} fusion(bf16[4,1032,256]{2,1,0:T(8,128)(2,1)S(1)} %pad_maximum_fusion, s32[1024]{0:T(1024)S(1)} %pad_clamp_fusion), kind=kCustom, calls=%fused_computation | custom fusion | bytes 4227088 | tf_op jit(solution)/shard_map/jit(_take)/gather | solution.py:154
  44.5 1.9 %select_bitcast_fusion = bf16[1032,4,256]{2,0,1:T(8,128)(2,1)S(1)} fusion(bf16[4,1032,256]{2,1,0:T(8,128)(2,1)} %gather_fusion, pred[4]{0:T(512)(128)(4,1)S(1)} %compare_and_fusion), kind=kLoop, calls=%fused_computation.23 | loop fusion | flops 1056768 | bytes 4227076 | tf_op jit(solution)/shard_map/jit(_take)/select_n | solution.py:154
  46.3 2.3 %slice_convert_fusion = f32[1024,4,256]{2,0,1:T(8,128)} fusion(bf16[1032,4,256]{2,0,1:T(8,128)(2,1)S(1)} %select_bitcast_fusion), kind=kLoop, calls=%fused_computation.24 | loop fusion | flops 1048576 | bytes 6291456 | tf_op jit(solution)/shard_map/convert_element_type | solution.py:156
  48.6 5.4 %copy.18 = f32[1024,4,256]{0,2,1:T(8,128)} copy(f32[1024,4,256]{2,0,1:T(8,128)} %slice_convert_fusion) | data formatting | bytes 8388608 | tf_op jit(solution)/shard_map/convert_element_type | solution.py:156
  54.0 0.5 multiply_reduce_fusion
  54.5 4.0 %fusion.7 = bf16[1024,1024]{0,1:T(8,128)(2,1)} fusion(f32[1024,4,256]{0,2,1:T(8,128)} %copy.18, f32[1024]{0:T(1024)S(1)} %bitcast.63, f32[1024]{0:T(1024)S(1)} %add_rsqrt_fusion), kind=kLoop, calls=%fused_computation.13 | loop fusion | flops 3145728 | bytes 6299648 | tf_op jit(solution)/shard_map/convert_element_type | solution.py:159
  58.5 26.9 %all-gather.3.cloned.1.call-done.w_ref = bf16[8192,1024]{1,0:T(8,128)(2,1)} async-done(((bf16[256,1024]{1,0:T(8,128)(2,1)}), bf16[8192,1024]{1,0:T(8,128)(2,1)}) %all-gather.3.cloned.1.call-update) | async-done | bytes 16777232 | tf_op jit(solution)/shard_map/all_gather | solution.py:169
  85.4 33.9 %shard_map.85 = (f32[1,1024]{1,0:T(1,128)}, f32[1,1024]{1,0:T(1,128)}, f32[1,1024]{1,0:T(1,128)}, f32[1,1024]{1,0:T(1,128)}) custom-call(bf16[8192,1024]{1,0:T(8,128)(2,1)} %all-gather.3.cloned.1.call-done.w_ref, bf16[1024,1024]{1,0:T(8,128)(2,1)} %bitcast.56, f32[8192,1]{1,0:T(8,128)} %fusion.13.b_ref, s32[8192,1]{1,0:T(8,128)} %fusion.5.v_ref, ...), custom_call_target="tpu_custom_call" | custom-call | flops 17179869184 | bytes 18874368 | tf_op jit(solution)/shard_map/pallas_call | solution.py:100
  119.3 0.7 fusion.24
  120.0 1.3 pad_maximum_fusion.1.x_ref
  121.3 7.4 %shard_map.86 = f32[4,4,1024]{2,1,0:T(4,128)} custom-call(f32[4,1024]{1,0:T(4,128)} %pad_maximum_fusion.1.x_ref), custom_call_target="tpu_custom_call" | custom-call | tf_op jit(solution)/shard_map/pallas_call | solution.py:40
  128.8 1.0 slice_bitcast_fusion.7
  129.8 0.7 slice_bitcast_fusion.2
  130.5 0.1 fusion.18
  130.6 0.7 fusion.26
  131.3 0.6 dynamic_slice.6
  131.9 0.6 dynamic_slice.7
  132.5 1.3 pad_maximum_fusion.2
  133.9 0.1 broadcast_multiply_fusion
  133.9 0.6 scatter.9.x_ref
  134.5 10.9 %shard_map.87 = f32[32,8,128]{2,1,0:T(8,128)} custom-call(f32[8,128]{1,0:T(8,128)} %scatter.9.x_ref), custom_call_target="tpu_custom_call" | custom-call | tf_op jit(solution)/shard_map/pallas_call | solution.py:40
  145.4 0.9 reduce_sum.93
  146.4 0.2 maximum_reduce_fusion
  146.6 0.1 slice_divide_fusion
  146.7 0.7 copy.19
  (6 shorter events, 0.1 us)
Async XLA Ops:
  7.2 78.3 %all-gather.3.cloned.1.call-start = ((), (), s32[]{:S(2)}) async-start(), calls=%async_computation | async-start | bytes 17301504 | tf_op jit(solution)/shard_map/all_gather | solution.py:169
  11.1 15.0 %collective-permute-start.1 = (bf16[1032,256]{1,0:T(8,128)(2,1)S(1)}, bf16[1032,256]{1,0:T(8,128)(2,1)S(1)}, u32[]{:S(2)}, u32[]{:S(2)}) collective-permute-start(bf16[1032,256]{1,0:T(8,128)(2,1)S(1)} %get-tuple-element.51), channel_id=1, source_target_pairs={{0,1},{1,2},{2,3},{3,0},{4,5},{5,6},{6,7},{7,4},{8,9},{9,10},{10,1... | collective-permute-start | bytes 1585160 | tf_op jit(solution)/shard_map/ppermute | solution.py:148
  12.8 20.1 %collective-permute-start = (bf16[1032,256]{1,0:T(8,128)(2,1)S(1)}, bf16[1032,256]{1,0:T(8,128)(2,1)S(1)}, u32[]{:S(2)}, u32[]{:S(2)}) collective-permute-start(bf16[1032,256]{1,0:T(8,128)(2,1)S(1)} %get-tuple-element.51), channel_id=1, source_target_pairs={{0,3},{1,0},{2,1},{3,2},{4,7},{5,4},{6,5},{7,6},{8,11},{9,8},{10,9... | collective-permute-start | bytes 1585160 | tf_op jit(solution)/shard_map/ppermute | solution.py:148
  26.1 14.0 %collective-permute-start.2 = (bf16[1032,256]{1,0:T(8,128)(2,1)S(1)}, bf16[1032,256]{1,0:T(8,128)(2,1)S(1)}, u32[]{:S(2)}, u32[]{:S(2)}) collective-permute-start(bf16[1032,256]{1,0:T(8,128)(2,1)S(1)} %collective-permute-done.1), channel_id=1, source_target_pairs={{0,1},{1,2},{2,3},{3,0},{4,5},{5,6},{6,7},{7,4},{8,9},{9,10},{10,1... | collective-permute-start | bytes 1585160 | tf_op jit(solution)/shard_map/ppermute | solution.py:148
  32.9 7.2 %copy-start = (bf16[1032,256]{1,0:T(8,128)(2,1)}, bf16[1032,256]{1,0:T(8,128)(2,1)S(1)}, u32[]{:S(2)}) copy-start(bf16[1032,256]{1,0:T(8,128)(2,1)S(1)} %collective-permute-done) | copy-start | bytes 1585156
  40.1 0.8 copy-start.1
Sparse Core Ops, SparseCore 0:
  10.2 75.1 all-gather.2
where the time goes:
time: 156 us; the launch traced here: 154 us
  Pallas kernels  52.2 us (33%)
  waiting for transfers between devices  43.6 us (28%)
  other arithmetic  24.8 us (16%)
  between operations  15.4 us (10%)
  local copies, waits for them, and re-layouts  14.3 us (9%)
  starting transfers between devices  3.82 us (2%)
    pallas_call x1, Pallas kernels, fused_stats(): pl.pallas_call(functools.partial(stats_kernel, grid[1]), out_shape=(stat,...  33.9 us
    all_gather x1, waiting for transfers between devices, body(): piece = lax.all_gather(part, REQ, axis=0, tiled=False)  26.9 us
    pallas_call x2, Pallas kernels, peer_gather(): pl.pallas_call(functools.partial(peer_kernel, n, coords_of), out_shape=ja...  18.4 us
    ppermute x3, waiting for transfers between devices, body(): lax.ppermute(x, 'x', [(i, (i + d) % splits) for i in range(splits)])  16.6 us
    convert_element_type x1, local copies, waits for them, and re-layouts, body(): widened = gathered[:rows].astype(jnp.float32)  5.41 us
    select_n x1, other arithmetic, body(): jnp.where(valid, (owner * splits + column_index) * shard_cols + offset, -1)  5 us
    convert_element_type x1, other arithmetic, body(): (widened * scale[:, None] * gain_full[None, :]).astype(jnp.bfloat16)  3.95 us
    ppermute x3, starting transfers between devices, body(): lax.ppermute(x, 'x', [(i, (i + d) % splits) for i in range(splits)])  3.78 us
  transfers between devices with their start and end apart: 4, of which 3 were waited for; matrix products, arithmetic and copies ran while one was open for 17% of the time, Pallas kernels for 0%

commit v1 on v0

--- a/solution.py
+++ b/solution.py
@@ -59,11 +59,15 @@
     return me, lambda t: (t // (zs * cs), (t // cs) % zs, t % cs, here[3])
 
 
-def stats_kernel(steps, w_ref, x_ref, b_ref, v_ref, t_ref, top_ref, tot_ref, mom_ref, pick_ref, m_sc, s_sc, mo_sc, p_sc):
+def stats_kernel(steps, n, w_ref, x_ref, b_ref, v_ref, t_ref, out_ref, m_sc, s_sc, mo_sc, p_sc, mine, held, send_sem, recv_sem):
     j = pl.program_id(1)
+    me, coords = along_x()
+    barrier = pltpu.get_barrier_semaphore()
 
     @pl.when(j == 0)
     def _():
+        for d in range(1, n):
+            pl.semaphore_signal(barrier, inc=1, device_id=coords((me + d) % n), device_id_type=pl.DeviceIdType.MESH)
         m_sc[...] = jnp.full(m_sc.shape, NEG, jnp.float32)
         s_sc[...] = jnp.zeros(s_sc.shape, jnp.float32)
         mo_sc[...] = jnp.zeros(mo_sc.shape, jnp.float32)
@@ -85,21 +89,32 @@
 
     @pl.when(j == steps - 1)
     def _():
-        top_ref[...] = m_sc[...]
-        tot_ref[...] = jnp.sum(s_sc[...], axis=0, keepdims=True)
-        mom_ref[...] = jnp.sum(mo_sc[...], axis=0, keepdims=True)
-        pick_ref[...] = jnp.sum(p_sc[...], axis=0, keepdims=True)
-
-
-def fused_stats(normed_t, piece, bias, vocab_ids, ids, tm=1024, tn=1024):
+        mine[0:1, :] = m_sc[...]
+        mine[1:2, :] = jnp.sum(s_sc[...], axis=0, keepdims=True)
+        mine[2:3, :] = jnp.sum(mo_sc[...], axis=0, keepdims=True)
+        mine[3:4, :] = jnp.sum(p_sc[...], axis=0, keepdims=True)
+        held[pl.ds(me, 1)] = mine[...][None]
+        pl.semaphore_wait(barrier, n - 1)
+        copies = []
+        for d in range(1, n):
+            c = pltpu.make_async_remote_copy(
+                src_ref=mine, dst_ref=held.at[me], send_sem=send_sem.at[d], recv_sem=recv_sem.at[d],
+                device_id=coords((me + d) % n), device_id_type=pl.DeviceIdType.MESH)
+            c.start()
+            copies.append(c)
+        for c in copies:
+            c.wait()
+        out_ref[...] = held[...]
+
+
+def fused_stats(normed_t, piece, bias, vocab_ids, ids, n, tm=1024, tn=1024):
     depth, rows = normed_t.shape
     cols = piece.shape[0]
     grid = (rows // tm, cols // tn)
-    stat = jax.ShapeDtypeStruct((1, rows), jnp.float32)
-    stat_spec = pl.BlockSpec((1, tm), lambda i, j: (0, i))
+    assert grid[0] == 1
     return pl.pallas_call(
-        functools.partial(stats_kernel, grid[1]),
-        out_shape=(stat, stat, stat, stat),
+        functools.partial(stats_kernel, grid[1], n),
+        out_shape=jax.ShapeDtypeStruct((n, 4, rows), jnp.float32),
         grid=grid,
         in_specs=[
             pl.BlockSpec((tn, depth), lambda i, j: (j, 0)),
@@ -108,9 +123,13 @@
             pl.BlockSpec((tn, 1), lambda i, j: (j, 0)),
             pl.BlockSpec((1, tm), lambda i, j: (0, i)),
         ],
-        out_specs=(stat_spec, stat_spec, stat_spec, stat_spec),
-        scratch_shapes=[pltpu.VMEM((1, tm), jnp.float32)] + [pltpu.VMEM((SUB, tm), jnp.float32)] * 3,
-        compiler_params=pltpu.CompilerParams(dimension_semantics=("arbitrary", "arbitrary")),
+        out_specs=pl.BlockSpec((n, 4, rows), lambda i, j: (0, 0, 0)),
+        scratch_shapes=[pltpu.VMEM((1, tm), jnp.float32)] + [pltpu.VMEM((SUB, tm), jnp.float32)] * 3
+        + [pltpu.VMEM((4, rows), jnp.float32), pltpu.VMEM((n, 4, rows), jnp.float32),
+           pltpu.SemaphoreType.DMA((n,)), pltpu.SemaphoreType.DMA((n,))],
+        compiler_params=pltpu.CompilerParams(
+            dimension_semantics=("arbitrary", "arbitrary"), collective_id=0, has_side_effects=True
+        ),
         cost_estimate=pl.CostEstimate(
             flops=2 * rows * cols * depth,
             transcendentals=rows * cols,
@@ -119,10 +138,9 @@
     )(piece, normed_t, bias, vocab_ids, ids)
 
 
-def chunk_stats(normed, piece, valid, vocab_ids, ids):
+def chunk_stats(normed, piece, valid, vocab_ids, ids, n):
     bias = jnp.where(valid, 0.0, NEG).astype(jnp.float32)[:, None]
-    top, total, moment, pick = fused_stats(normed.T, piece, bias, vocab_ids[:, None], ids[None, :])
-    return top[0], total[0], moment[0], pick[0]
+    return fused_stats(normed.T, piece, bias, vocab_ids[:, None], ids[None, :], n)
 
 
 def merge(stats):
@@ -174,10 +192,9 @@
         offset = lo + g % chunk
         valid = offset < hi
         vocab_ids = jnp.where(valid, (owner * splits + column_index) * shard_cols + offset, -1)
-        stats.append(chunk_stats(normed, piece, valid, vocab_ids, token_ids))
-    mine = merge(stats)
-
-    everyone = peer_gather(jnp.stack(mine), splits, along_x, 0)
+        stats.append(chunk_stats(normed, piece, valid, vocab_ids, token_ids, splits))
+    everyone = stats[0]
+
     top, total, moment, picked = merge([tuple(everyone[k, j] for j in range(4)) for k in range(splits)])
 
     positions = jnp.arange(rows, dtype=jnp.int32)

time: 156 us -> 151 us (0.968)
  Pallas kernels: 52.2 us -> 49.7 us
  other arithmetic: 24.8 us -> 22.8 us
    pallas_call x2 -> x1, Pallas kernels: 18.4 us -> 10.9 us  [peer_gather(): pl.pallas_call(functools.partial(peer_kernel, n, coords_of), out_shape=ja...]
    pallas_call x1, Pallas kernels: 33.9 us -> 38.8 us  [fused_stats(): pl.pallas_call(functools.partial(stats_kernel, grid[1], n), out_shape=jax...]
  transfers between devices with their start and end apart: 4 -> 4, of which waited for: 3 -> 3; matrix products, arithmetic and copies ran while one was open for 17% -> 18% of each run, Pallas kernels for 0% -> 0%
where the time goes in v1:
time: 151 us; the launch traced here: 150 us
  Pallas kernels  49.7 us (33%)
  waiting for transfers between devices  43.6 us (29%)
  other arithmetic  22.8 us (15%)
  between operations  15.4 us (10%)
  local copies, waits for them, and re-layouts  14.3 us (9%)
  starting transfers between devices  3.82 us (3%)
    pallas_call x1, Pallas kernels, fused_stats(): pl.pallas_call(functools.partial(stats_kernel, grid[1], n), out_shape=jax...  38.8 us
    all_gather x1, waiting for transfers between devices, body(): piece = lax.all_gather(part, REQ, axis=0, tiled=False)  26.9 us
    ppermute x3, waiting for transfers between devices, body(): lax.ppermute(x, 'x', [(i, (i + d) % splits) for i in range(splits)])  16.6 us
    pallas_call x1, Pallas kernels, peer_gather(): pl.pallas_call(functools.partial(peer_kernel, n, coords_of), out_shape=ja...  10.9 us
    convert_element_type x1, local copies, waits for them, and re-layouts, body(): widened = gathered[:rows].astype(jnp.float32)  5.41 us
    select_n x1, other arithmetic, body(): jnp.where(valid, (owner * splits + column_index) * shard_cols + offset, -1)  5 us
    convert_element_type x1, other arithmetic, body(): (widened * scale[:, None] * gain_full[None, :]).astype(jnp.bfloat16)  3.95 us
    ppermute x3, starting transfers between devices, body(): lax.ppermute(x, 'x', [(i, (i + d) % splits) for i in range(splits)])  3.78 us
  transfers between devices with their start and end apart: 4, of which 3 were waited for; matrix products, arithmetic and copies ran while one was open for 18% of the time, Pallas kernels for 0%

profile of v1, /device:TPU:0, one launch (start us, length us, event | category | flops | bytes accessed | tf_op | source)
XLA Modules:
  0.0 149.7 jit_solution(9951204561398239746)
XLA Ops:
  7.2 0.0 all-gather.3.cloned.1.call-start
  7.2 1.2 copy.17
  8.5 0.8 concatenate.10
  9.3 0.0 all-gather.3.cloned.1.call-update
  9.3 0.7 reshape.249
  10.0 1.1 fusion.23
  11.1 1.7 %collective-permute-start.1 = (bf16[1032,256]{1,0:T(8,128)(2,1)S(1)}, bf16[1032,256]{1,0:T(8,128)(2,1)S(1)}, u32[]{:S(2)}, u32[]{:S(2)}) collective-permute-start(bf16[1032,256]{1,0:T(8,128)(2,1)S(1)} %get-tuple-element.43), channel_id=1, source_target_pairs={{0,1},{1,2},{2,3},{3,0},{4,5},{5,6},{6,7},{7,4},{8,9},{9,10},{10,1... | collective-permute-start | bytes 1585160 | tf_op jit(solution)/shard_map/ppermute | solution.py:166
  12.8 1.6 %collective-permute-start = (bf16[1032,256]{1,0:T(8,128)(2,1)S(1)}, bf16[1032,256]{1,0:T(8,128)(2,1)S(1)}, u32[]{:S(2)}, u32[]{:S(2)}) collective-permute-start(bf16[1032,256]{1,0:T(8,128)(2,1)S(1)} %get-tuple-element.43), channel_id=1, source_target_pairs={{0,3},{1,0},{2,1},{3,2},{4,7},{5,4},{6,5},{7,6},{8,11},{9,8},{10,9... | collective-permute-start | bytes 1585160 | tf_op jit(solution)/shard_map/ppermute | solution.py:166
  14.4 2.2 %fusion.13.b_ref = f32[8192,1]{1,0:T(8,128)} fusion(), kind=kLoop, calls=%fused_computation.21 | loop fusion | flops 65536 | bytes 32768 | tf_op jit(solution)/shard_map/jit(_where)/select_n | solution.py:142
  16.6 9.4 %collective-permute-done.1 = bf16[1032,256]{1,0:T(8,128)(2,1)S(1)} collective-permute-done((bf16[1032,256]{1,0:T(8,128)(2,1)S(1)}, bf16[1032,256]{1,0:T(8,128)(2,1)S(1)}, u32[]{:S(2)}, u32[]{:S(2)}) %collective-permute-start.1) | collective-permute-done | bytes 528416 | tf_op jit(solution)/shard_map/ppermute | solution.py:166
  26.1 0.5 collective-permute-start.2
  26.5 5.0 %fusion.5.v_ref = s32[8192,1]{1,0:T(8,128)} fusion(s32[]{:T(128)S(6)} %axis_index.12), kind=kLoop, calls=%fused_computation.10 | loop fusion | flops 147456 | bytes 32772 | tf_op jit(solution)/shard_map/jit(_where)/select_n | solution.py:194
  32.9 0.0 collective-permute-done
  32.9 0.0 copy-start
  32.9 7.2 %collective-permute-done.2 = bf16[1032,256]{1,0:T(8,128)(2,1)S(1)} collective-permute-done((bf16[1032,256]{1,0:T(8,128)(2,1)S(1)}, bf16[1032,256]{1,0:T(8,128)(2,1)S(1)}, u32[]{:S(2)}, u32[]{:S(2)}) %collective-permute-start.2) | collective-permute-done | bytes 528416 | tf_op jit(solution)/shard_map/ppermute | solution.py:166
  40.1 0.0 copy-start.1
  40.1 0.0 copy-done
  40.1 0.8 copy-done.1
  40.9 1.5 pad_maximum_fusion
  42.4 2.1 %gather_fusion = bf16[4,1032,256]{2,1,0:T(8,128)(2,1)} fusion(bf16[4,1032,256]{2,1,0:T(8,128)(2,1)S(1)} %pad_maximum_fusion, s32[1024]{0:T(1024)S(1)} %pad_clamp_fusion), kind=kCustom, calls=%fused_computation | custom fusion | bytes 4227088 | tf_op jit(solution)/shard_map/jit(_take)/gather | solution.py:172
  44.5 1.9 %select_bitcast_fusion = bf16[1032,4,256]{2,0,1:T(8,128)(2,1)S(1)} fusion(bf16[4,1032,256]{2,1,0:T(8,128)(2,1)} %gather_fusion, pred[4]{0:T(512)(128)(4,1)S(1)} %compare_and_fusion), kind=kLoop, calls=%fused_computation.23 | loop fusion | flops 1056768 | bytes 4227076 | tf_op jit(solution)/shard_map/jit(_take)/select_n | solution.py:172
  46.3 2.3 %slice_convert_fusion = f32[1024,4,256]{2,0,1:T(8,128)} fusion(bf16[1032,4,256]{2,0,1:T(8,128)(2,1)S(1)} %select_bitcast_fusion), kind=kLoop, calls=%fused_computation.24 | loop fusion | flops 1048576 | bytes 6291456 | tf_op jit(solution)/shard_map/convert_element_type | solution.py:174
  48.6 5.4 %copy.18 = f32[1024,4,256]{0,2,1:T(8,128)} copy(f32[1024,4,256]{2,0,1:T(8,128)} %slice_convert_fusion) | data formatting | bytes 8388608 | tf_op jit(solution)/shard_map/convert_element_type | solution.py:174
  54.0 0.5 multiply_reduce_fusion
  54.5 4.0 %fusion.7 = bf16[1024,1024]{0,1:T(8,128)(2,1)} fusion(f32[1024,4,256]{0,2,1:T(8,128)} %copy.18, f32[1024]{0:T(1024)S(1)} %bitcast.63, f32[1024]{0:T(1024)S(1)} %add_rsqrt_fusion), kind=kLoop, calls=%fused_computation.13 | loop fusion | flops 3145728 | bytes 6299648 | tf_op jit(solution)/shard_map/convert_element_type | solution.py:177
  58.5 26.9 %all-gather.3.cloned.1.call-done.w_ref = bf16[8192,1024]{1,0:T(8,128)(2,1)} async-done(((bf16[256,1024]{1,0:T(8,128)(2,1)}), bf16[8192,1024]{1,0:T(8,128)(2,1)}) %all-gather.3.cloned.1.call-update) | async-done | bytes 16777232 | tf_op jit(solution)/shard_map/all_gather | solution.py:187
  85.4 38.8 %shard_map.85 = f32[4,4,1024]{2,1,0:T(4,128)} custom-call(bf16[8192,1024]{1,0:T(8,128)(2,1)} %all-gather.3.cloned.1.call-done.w_ref, bf16[1024,1024]{1,0:T(8,128)(2,1)} %bitcast.56, f32[8192,1]{1,0:T(8,128)} %fusion.13.b_ref, s32[8192,1]{1,0:T(8,128)} %fusion.5.v_ref, s32[1,1024]{1,0:T(1,128)} %bitcast.65), custom_call_target="tpu_custom_call" | custom-call | flops 17179869184 | bytes 18874368 | tf_op jit(solution)/shard_map/pallas_call | solution.py:115
  124.3 1.0 slice_bitcast_fusion.7
  125.3 0.7 slice_bitcast_fusion.2
  126.0 0.1 fusion.18
  126.1 0.7 fusion.24
  126.8 0.6 dynamic_slice.6
  127.4 0.6 dynamic_slice.7
  128.1 1.3 pad_maximum_fusion.1
  129.4 0.1 broadcast_multiply_fusion
  129.5 0.6 scatter.9.x_ref
  130.1 10.9 %shard_map.86 = f32[32,8,128]{2,1,0:T(8,128)} custom-call(f32[8,128]{1,0:T(8,128)} %scatter.9.x_ref), custom_call_target="tpu_custom_call" | custom-call | tf_op jit(solution)/shard_map/pallas_call | solution.py:40
  141.0 0.9 reduce_sum.81
  141.9 0.2 maximum_reduce_fusion
  142.1 0.1 slice_divide_fusion
  142.2 0.7 copy.19
  (6 shorter events, 0.1 us)
Async XLA Ops:
  7.2 78.3 %all-gather.3.cloned.1.call-start = ((), (), s32[]{:S(2)}) async-start(), calls=%async_computation | async-start | bytes 17301504 | tf_op jit(solution)/shard_map/all_gather | solution.py:187
  11.1 15.0 %collective-permute-start.1 = (bf16[1032,256]{1,0:T(8,128)(2,1)S(1)}, bf16[1032,256]{1,0:T(8,128)(2,1)S(1)}, u32[]{:S(2)}, u32[]{:S(2)}) collective-permute-start(bf16[1032,256]{1,0:T(8,128)(2,1)S(1)} %get-tuple-element.43), channel_id=1, source_target_pairs={{0,1},{1,2},{2,3},{3,0},{4,5},{5,6},{6,7},{7,4},{8,9},{9,10},{10,1... | collective-permute-start | bytes 1585160 | tf_op jit(solution)/shard_map/ppermute | solution.py:166
  12.8 20.1 %collective-permute-start = (bf16[1032,256]{1,0:T(8,128)(2,1)S(1)}, bf16[1032,256]{1,0:T(8,128)(2,1)S(1)}, u32[]{:S(2)}, u32[]{:S(2)}) collective-permute-start(bf16[1032,256]{1,0:T(8,128)(2,1)S(1)} %get-tuple-element.43), channel_id=1, source_target_pairs={{0,3},{1,0},{2,1},{3,2},{4,7},{5,4},{6,5},{7,6},{8,11},{9,8},{10,9... | collective-permute-start | bytes 1585160 | tf_op jit(solution)/shard_map/ppermute | solution.py:166
  26.1 14.0 %collective-permute-start.2 = (bf16[1032,256]{1,0:T(8,128)(2,1)S(1)}, bf16[1032,256]{1,0:T(8,128)(2,1)S(1)}, u32[]{:S(2)}, u32[]{:S(2)}) collective-permute-start(bf16[1032,256]{1,0:T(8,128)(2,1)S(1)} %collective-permute-done.1), channel_id=1, source_target_pairs={{0,1},{1,2},{2,3},{3,0},{4,5},{5,6},{6,7},{7,4},{8,9},{9,10},{10,1... | collective-permute-start | bytes 1585160 | tf_op jit(solution)/shard_map/ppermute | solution.py:166
  32.9 7.2 %copy-start = (bf16[1032,256]{1,0:T(8,128)(2,1)}, bf16[1032,256]{1,0:T(8,128)(2,1)S(1)}, u32[]{:S(2)}) copy-start(bf16[1032,256]{1,0:T(8,128)(2,1)S(1)} %collective-permute-done) | copy-start | bytes 1585156
  40.1 0.8 copy-start.1
Sparse Core Ops, SparseCore 0:
  10.2 75.1 all-gather.2
